TPU v7x, 128 devices: a whole 4x4x4 slice. The times are simulated.
128 devices in a mesh: gx: 16 (over z, x_hi, core), gy: 8 (over x_lo, y).
Axes of the slice: x: 4 (x_hi: 2, x_lo: 2; x = x_hi * 2 + x_lo), y: 4, z: 4, core: 2. Of those that a mesh axis runs over, the one named last changes fastest.
Arguments:
- grid_field: bfloat16 [1, 20, 2048, 2048], P(None, None, 'gx', 'gy'), may hold values from -8 to 8
- spectral_weight: float32 [2, 2, 20, 20, 2048], P(None, None, None, None, ('gx', 'gy')), may hold values from -1 to 1
- conv_near: bfloat16 [2, 20, 180], replicated, may hold values from -0.4375 to 0.4375
- conv_far: bfloat16 [2, 20, 500], replicated, may hold values from -0.25 to 0.25
- mix_logits: float32 [2, 3], replicated, may hold values from -1 to 1
- channel_bias: float32 [2, 20], replicated, may hold values from -3 to 3
Outputs:
- result_field: bfloat16 [1, 20, 2048, 2048], P(None, None, 'gx', 'gy')
All inputs are finite; a program needn't handle non-finite values.
Results may differ from a plain program's by a relative error of at most 0.004.
Values may be sent and summed in bfloat16 or wider, within the bound.
No kernel may reach another device: no remote copies, remote signals or barrier semaphores. Data moves between devices by JAX's collectives and lax.ppermute only.
A program may use at most 192 MiB of HBM per device.

v0:
```python
import math
import jax
import jax.numpy as jnp
from jax import lax
from jax.sharding import PartitionSpec as P

NX = 2048
NY = 2048
MX = 32
MY = 32
LAYERS = 2
KX = 64
MODES = 2048
full_turn = 2.0 * math.pi
highest = lax.Precision.HIGHEST


def padded_2(value, sides, width):
    for axis, dim in sides:
        size, length = (lax.axis_size(axis), value.shape[dim])
        up = [(i, (i + 1) % size) for i in range(size)]
        down = [(j, i) for i, j in up]
        last = lax.slice_in_dim(value, length - width, length, axis=dim)
        first = lax.slice_in_dim(value, 0, width, axis=dim)
        before = lax.ppermute(last, axis, up)
        after = lax.ppermute(first, axis, down)
        value = jnp.concatenate([before, value, after], axis=dim)
    return value


def forward_table(positions):
    col_modes = jnp.arange(MY, dtype=jnp.int32)
    phases = (positions[:, None] * col_modes[None, :] % NY).astype(jnp.float32) * (full_turn / NY)
    return jnp.concatenate([jnp.cos(phases), -jnp.sin(phases)], axis=1).astype(jnp.bfloat16)


def row_tables(positions):
    lower = jnp.arange(MX, dtype=jnp.int32)
    row_modes = jnp.concatenate([lower, lower + (NX - MX)])
    phases = (positions[:, None] * row_modes[None, :] % NX).astype(jnp.float32) * (full_turn / NX)
    return (jnp.cos(phases), jnp.sin(phases))


def inverse_table(positions):
    col_modes = jnp.arange(MY, dtype=jnp.int32)
    col_weight = jnp.where(col_modes == 0, 1.0, 2.0).astype(jnp.float32) / (NX * NY)
    phases = (col_modes[:, None] * positions[None, :] % NY).astype(jnp.float32) * (full_turn / NY)
    return jnp.concatenate(
        [jnp.cos(phases) * col_weight[:, None], -jnp.sin(phases) * col_weight[:, None]], axis=0
    )


def conv_rows(padded_plane, tap_weights, dilation, side_taps, first_row, count_rows, local_cols):
    channels = padded_plane.shape[0]
    pieces = []
    for row_tap in range(side_taps):
        for col_tap in range(side_taps):
            row_offset = 4 + (row_tap - side_taps // 2) * dilation + first_row
            col_offset = 4 + (col_tap - side_taps // 2) * dilation
            pieces.append(
                padded_plane[
                    :, row_offset : row_offset + count_rows, col_offset : col_offset + local_cols
                ]
            )
    stacked = jnp.stack(pieces, 0)
    shaped_weights = tap_weights.reshape(channels, side_taps * side_taps, channels)
    return jnp.einsum("otc,tcxy->oxy", shaped_weights, stacked, preferred_element_type=jnp.float32)


def on_device(grid_field, spectral_weight, conv_near, conv_far, mix_logits, channel_bias):
    channels = grid_field.shape[1]
    local_rows = grid_field.shape[2]
    local_cols = grid_field.shape[3]
    row_positions = lax.axis_index("gx") * local_rows + jnp.arange(local_rows, dtype=jnp.int32)
    col_positions = lax.axis_index("gy") * local_cols + jnp.arange(local_cols, dtype=jnp.int32)
    forward_cols = forward_table(col_positions)
    cosine_rows, sine_rows = row_tables(row_positions)
    inverse_cols = inverse_table(col_positions)
    share_modes = spectral_weight.shape[-1]
    owner_index = lax.axis_index("gx") * lax.axis_size("gy") + lax.axis_index("gy")
    mode_start = owner_index * share_modes
    row_blocks = max(1, local_rows // 32)
    while local_rows % row_blocks != 0:
        row_blocks = row_blocks - 1
    block_rows = local_rows // row_blocks
    planes_block = grid_field
    for layer_index in range(LAYERS):
        planes_here = planes_block.shape[0]
        line_sums = jnp.dot(
            planes_block.reshape(planes_here * channels * local_rows, local_cols),
            forward_cols,
            preferred_element_type=jnp.float32,
        )
        line_sums = line_sums.reshape(planes_here, channels, local_rows, 2 * MY)
        real_lines = line_sums[..., :MY]
        imaginary_lines = line_sums[..., MY:]

        def contract_rows(operand, lookup):
            return jnp.einsum("pcxk,xj->pcjk", operand, lookup, precision=highest)

        real_spec = contract_rows(real_lines, cosine_rows) + contract_rows(
            imaginary_lines, sine_rows
        )
        imaginary_spec = contract_rows(imaginary_lines, cosine_rows) - contract_rows(
            real_lines, sine_rows
        )
        partial_value = jnp.stack(
            [
                real_spec.reshape(planes_here, channels, MODES),
                imaginary_spec.reshape(planes_here, channels, MODES),
            ]
        )
        totals = lax.psum(partial_value, ("gx", "gy"))
        own_modes = lax.dynamic_slice_in_dim(totals, mode_start, share_modes, 3)

        def mix_modes(spectrum, weights):
            return jnp.einsum("pcm,com->pom", spectrum, weights, precision=highest)

        weight_real = spectral_weight[layer_index, 0]
        weight_imaginary = spectral_weight[layer_index, 1]
        real_mixed = mix_modes(own_modes[0], weight_real) - mix_modes(
            own_modes[1], weight_imaginary
        )
        imaginary_mixed = mix_modes(own_modes[1], weight_real) + mix_modes(
            own_modes[0], weight_imaginary
        )
        own_block = jnp.stack([real_mixed, imaginary_mixed])[None]
        gathered = lax.all_gather(own_block, ("gx", "gy"), axis=0, tiled=True)
        gathered = jnp.transpose(gathered, (1, 2, 3, 0, 4)).reshape(2, planes_here, channels, MODES)
        real_full = gathered[0].reshape(planes_here, channels, KX, MY)
        imaginary_full = gathered[1].reshape(planes_here, channels, KX, MY)

        def expand_rows(spectrum, lookup):
            return jnp.einsum("pcjk,xj->pcxk", spectrum, lookup, precision=highest)

        real_rows = expand_rows(real_full, cosine_rows) - expand_rows(imaginary_full, sine_rows)
        imaginary_rows = expand_rows(real_full, sine_rows) + expand_rows(
            imaginary_full, cosine_rows
        )
        stacked = jnp.concatenate([real_rows, imaginary_rows], axis=-1).reshape(
            planes_here * channels * local_rows, 2 * MY
        )
        spectral = jnp.dot(stacked, inverse_cols, precision=highest)
        layer_spectral = spectral.reshape(planes_here, channels, local_rows, local_cols)
        padded = padded_2(planes_block, (("gx", 2), ("gy", 3)), 4)
        exponents = jnp.exp(mix_logits[layer_index])
        mixture = exponents / jnp.sum(exponents)
        bias_column = channel_bias[layer_index][:, None, None]
        row_pieces = []
        for block_index in range(row_blocks):
            first_row = block_index * block_rows
            near_term = conv_rows(
                padded[0], conv_near[layer_index], 1, 3, first_row, block_rows, local_cols
            )
            far_term = conv_rows(
                padded[0], conv_far[layer_index], 2, 5, first_row, block_rows, local_cols
            )
            spectral_rows = layer_spectral[0, :, first_row : first_row + block_rows, :]
            summed = (
                mixture[0] * spectral_rows
                + mixture[1] * near_term
                + mixture[2] * far_term
                + bias_column
            )
            row_pieces.append(jax.nn.gelu(summed, approximate=False).astype(jnp.bfloat16))
        outputs = [jnp.concatenate(row_pieces, axis=1)]
        planes_block = jnp.stack(outputs)
    return planes_block


def solution(mesh):
    in_specs = (
        P(None, None, "gx", "gy"),
        P(None, None, None, None, ("gx", "gy")),
        P(),
        P(),
        P(),
        P(),
    )
    out_specs = P(None, None, "gx", "gy")
    return jax.shard_map(
        on_device, mesh=mesh, in_specs=in_specs, out_specs=out_specs, check_vma=False
    )
```

profile of v0, /device:TPU:0, one launch (start us, length us, event | category | flops | bytes accessed | tf_op | source)
XLA Modules:
  0.0 1025.7 jit_solution(15079216024907753427)
XLA Ops:
  8.8 6.0 collective-permute-start.1
  37.3 2.9 collective-permute-start.3
  71.0 3.8 copy-done.15
  74.8 14.7 %constant_dynamic-update-slice_fusion.20 = (bf16[25,20,32,256]{3,1,2,0:T(8,128)(2,1)}, bf16[25,20,32,256]{3,1,2,0:T(8,128)(2,1)S(1)}, bf16[9,20,32,256]{3,1,2,0:...) fusion(bf16[25,20,32,256]{3,1,2,0:T(8,128)(2,1)} %get-tuple-ele, ...), kind=kLoop, calls=%fused_computation.275 | loop fusion | bytes 5505024
  109.3 6.5 convolution_bitcast_fusion.7
  124.9 39.9 %all-reduce.3.cloned.1.call-done = f32[2,1,20,2048]{3,0,2,1:T(2,128)} async-done(((f32[2,1,20,2048]{3,0,2,1:T(2,128)}), f32[2,1,20,2048]{3,0,2,1:T(2,128)}) %all-reduce.3.cloned.1.call-update) | async-done | bytes 327696 | tf_op jit(solution)/shard_map/psum | solution.py:113
  167.1 326.2 %all-gather = f32[256,1,20,16]{2,3,1,0:T(8,128)S(1)} all-gather(f32[2,1,20,16]{2,3,1,0:T(8,128)S(1)} %pad_maximum_fusion.8), channel_id=2, replica_groups=mesh['gx'=16,'gy'=8] {'gx','gy'}, dimensions={0}, use_global_device_ids=true | all-gather | bytes 330240 | tf_op jit(solution)/shard_map/all_gather | solution.py:128
  503.2 10.4 %fusion.42 = (bf16[20,32,256]{2,1,0:T(8,128)(2,1)S(1)}, bf16[20,32,256]{2,1,0:T(8,128)(2,1)S(1)}, bf16[20,32,256]{2,1,0:T(8,128)(2,1)S(1)}, bf16[20,32,256]{2,1,0:T(8,128)(2,1)S(1)}) fusion(f32[32,256,20]{1,2,0:T(8,128)} %convolution_bitcast_fusion.9, f32[32,256,20]{1,2,0:T(8,128)} %convolution_bitcast_fusion.10, ...), kind=kLoop, calls=%fused_computation.51 | loop fusion | flops 46530560 | bytes 9175132 | tf_op jit(solution)/shard_map/convert_element_type | solution.py:165
  516.9 5.3 collective-permute-start.5
  526.1 4.3 collective-permute-start.7
  548.7 3.2 copy-done.18
  554.4 2.9 constant_dynamic-update-slice_fusion.146
  557.2 2.7 constant_dynamic-update-slice_fusion.145
  560.0 2.6 constant_dynamic-update-slice_fusion.144
  562.6 2.9 constant_dynamic-update-slice_fusion.143
  576.2 2.8 copy-done.16
  579.2 4.5 fusion.25
  583.7 9.6 fusion.19
  593.3 5.3 fusion.22
  598.6 5.3 fusion.16
  606.4 2.8 fusion.31
  614.3 58.0 %all-reduce.5.cloned.1.call-done = f32[2,1,20,2048]{3,0,2,1:T(2,128)} async-done(((f32[2,1,20,2048]{3,0,2,1:T(2,128)}), f32[2,1,20,2048]{3,0,2,1:T(2,128)}) %all-reduce.5.cloned.1.call-update) | async-done | bytes 327696 | tf_op jit(solution)/shard_map/psum | solution.py:113
  674.7 325.8 %all-gather.1 = f32[256,1,20,16]{2,3,1,0:T(8,128)S(1)} all-gather(f32[2,1,20,16]{2,3,1,0:T(8,128)S(1)} %pad_maximum_fusion.9), channel_id=3, replica_groups=mesh['gx'=16,'gy'=8] {'gx','gy'}, dimensions={0}, use_global_device_ids=true | all-gather | bytes 330240 | tf_op jit(solution)/shard_map/all_gather | solution.py:128
  1006.8 10.5 %fusion.54 = (bf16[20,32,256]{2,1,0:T(8,128)(2,1)S(1)}, bf16[20,32,256]{2,1,0:T(8,128)(2,1)S(1)}, bf16[20,32,256]{2,1,0:T(8,128)(2,1)S(1)}, bf16[20,32,256]{2,1,0:T(8,128)(2,1)S(1)}) fusion(f32[32,256,20]{1,2,0:T(8,128)} %fusion.16, f32[32,256,20]{1,2,0:T(8,128)} %fusion.28, f32[1,20,128,256]{3,2,1,0:T(8,128)S(1)} %convolution_bitcast_fusion.1, ...), kind=kLoop, calls=%fused_computation.63 | loop fusion | flops 46530560 | bytes 9175132 | tf_op jit(solution)/shard_map/convert_element_type | solution.py:165
  (249 shorter events, 152.1 us)
Async XLA Ops:
  6.5 15.6 %copy-start.8 = (bf16[2,20,500]{2,0,1:T(2,128)(2,1)S(1)}, bf16[2,20,500]{2,0,1:T(2,128)(2,1)}, u32[]{:S(2)}) copy-start(bf16[2,20,500]{2,0,1:T(2,128)(2,1)} %param.9) | copy-start | bytes 120004
  6.5 158.2 %all-reduce.3.cloned.1.call-start = ((), (), s32[]{:S(2)}) async-start(), calls=%async_computation | async-start | bytes 655360 | tf_op jit(solution)/shard_map/psum | solution.py:113
  8.1 23.0 %collective-permute-start = (bf16[1,20,4,256]{3,1,2,0:T(8,128)(2,1)}, bf16[1,20,4,256]{3,1,2,0:T(8,128)(2,1)}, u32[]{:S(2)}, u32[]{:S(2)}) collective-permute-start(bf16[1,20,4,256]{3,1,2,0:T(8,128)(2,1)} %copy.500), channel_id=1, source_target_pairs={{0,8},{8,16},{16,24},{24,32},{32,40},{40,48},{48,56},{56,64},{64,7... | collective-permute-start | bytes 122888 | tf_op jit(solution)/shard_map/ppermute | solution.py:25
  8.8 24.0 %collective-permute-start.1 = (bf16[1,20,4,256]{3,1,2,0:T(8,128)(2,1)}, bf16[1,20,4,256]{3,1,2,0:T(8,128)(2,1)}, u32[]{:S(2)}, u32[]{:S(2)}) collective-permute-start(bf16[1,20,4,256]{3,1,2,0:T(8,128)(2,1)} %copy.501), channel_id=1, source_target_pairs={{8,0},{16,8},{24,16},{32,24},{40,32},{48,40},{56,48},{64,56},{72,6... | collective-permute-start | bytes 122888 | tf_op jit(solution)/shard_map/ppermute | solution.py:26
  15.0 10.7 %copy-start.19 = (f32[2,3]{1,0:T(2,128)S(1)}, f32[2,3]{1,0:T(2,128)}, u32[]{:S(2)}) copy-start(f32[2,3]{1,0:T(2,128)} %param.10) | copy-start | bytes 76
  15.0 17.0 %copy-start = (bf16[1,20,128,256]{3,2,1,0:T(8,128)(2,1)S(1)}, bf16[1,20,128,256]{3,2,1,0:T(8,128)(2,1)}, u32[]{:S(2)}) copy-start(bf16[1,20,128,256]{3,2,1,0:T(8,128)(2,1)} %param.6) | copy-start | bytes 3932164
  22.1 650.2 %all-reduce.5.cloned.1.call-start = ((), (), s32[]{:S(2)}) async-start(), calls=%async_computation.1 | async-start | bytes 655360 | tf_op jit(solution)/shard_map/psum | solution.py:113
  35.1 12.2 %collective-permute-start.2 = (bf16[1,20,136,4]{2,3,1,0:T(4,128)(2,1)}, bf16[1,20,136,4]{2,3,1,0:T(4,128)(2,1)S(1)}, u32[]{:S(2)}, u32[]{:S(2)}) collective-permute-start(bf16[1,20,136,4]{2,3,1,0:T(4,128)(2,1)} %copy.211), channel_id=1, source_target_pairs={{0,1},{1,2},{2,3},{3,4},{4,5},{5,6},{6,7},{7,0},{8,9},{9,10},{10,1... | collective-permute-start | bytes 65288 | tf_op jit(solution)/shard_map/ppermute | solution.py:25
  37.3 10.6 %collective-permute-start.3 = (bf16[1,20,136,4]{2,3,1,0:T(4,128)(2,1)S(1)}, bf16[1,20,136,4]{2,3,1,0:T(4,128)(2,1)}, u32[]{:S(2)}, u32[]{:S(2)}) collective-permute-start(bf16[1,20,136,4]{2,3,1,0:T(4,128)(2,1)S(1)} %copy.212), channel_id=1, source_target_pairs={{1,0},{2,1},{3,2},{4,3},{5,4},{6,5},{7,6},{0,7},{9,8},{10,9},{11,1... | collective-permute-start | bytes 65288 | tf_op jit(solution)/shard_map/ppermute | solution.py:26
  120.4 45.4 %copy-start.4 = (f32[20,20,16]{1,2,0:T(8,128)S(1)}, f32[20,20,16]{1,2,0:T(8,128)}, u32[]{:S(2)}) copy-start(f32[20,20,16]{1,2,0:T(8,128)} %get-tuple-element.287) | copy-start | bytes 76804
  120.4 46.1 %copy-start.3 = (f32[20,20,16]{1,2,0:T(8,128)S(1)}, f32[20,20,16]{1,2,0:T(8,128)}, u32[]{:S(2)}) copy-start(f32[20,20,16]{1,2,0:T(8,128)} %get-tuple-element.286) | copy-start | bytes 76804
  124.9 376.1 %copy-start.6 = (f32[32,256]{1,0:T(8,128)S(1)}, f32[32,256]{1,0:T(8,128)}, u32[]{:S(2)}) copy-start(f32[32,256]{1,0:T(8,128)} %get-tuple-element.296) | copy-start | bytes 98308
  167.1 336.1 %copy-start.21 = (f32[20]{0:T(128)S(1)}, f32[20]{0:T(128)}, u32[]{:S(2)}) copy-start(f32[20]{0:T(128)} %get-tuple-element.300) | copy-start | bytes 244
  494.2 9.0 copy-start.1
  500.9 12.8 %copy-start.12 = (bf16[256,32]{0,1:T(8,128)(2,1)S(1)}, bf16[256,32]{0,1:T(8,128)(2,1)}, u32[]{:S(2)}) copy-start(bf16[256,32]{0,1:T(8,128)(2,1)} %copy-done.11) | copy-start | bytes 49156
  500.9 12.8 %copy-start.14 = (bf16[256,32]{0,1:T(8,128)(2,1)S(1)}, bf16[256,32]{0,1:T(8,128)(2,1)}, u32[]{:S(2)}) copy-start(bf16[256,32]{0,1:T(8,128)(2,1)} %copy-done.13) | copy-start | bytes 49156
  516.8 7.1 collective-permute-start.4
  516.9 7.0 collective-permute-start.5
  525.6 6.2 collective-permute-start.6
  526.1 6.0 collective-permute-start.7
  568.1 11.1 %copy-start.9 = (bf16[20,25,20]{1,0,2:T(8,128)(2,1)S(1)}, bf16[20,25,20]{1,0,2:T(8,128)(2,1)}, u32[]{:S(2)}) copy-start(bf16[20,25,20]{1,0,2:T(8,128)(2,1)} %copy.257) | copy-start | bytes 60004
  583.7 9.6 copy-start.17
  606.4 66.9 %copy-start.2 = (f32[20,20,16]{1,2,0:T(8,128)S(1)}, f32[20,20,16]{1,2,0:T(8,128)}, u32[]{:S(2)}) copy-start(f32[20,20,16]{1,2,0:T(8,128)} %get-tuple-element.285) | copy-start | bytes 76804
  674.7 332.2 %copy-start.20 = (f32[20]{0:T(128)S(1)}, f32[20]{0:T(128)}, u32[]{:S(2)}) copy-start(f32[20]{0:T(128)} %get-tuple-element.299) | copy-start | bytes 244
  (11 other events, 61.0 us)
Sparse Core Ops, SparseCore 0:
  22.2 142.4 all-reduce.2
  531.7 140.5 all-reduce.4
where the time goes:
time: 1030 us
  blocking collectives  652 us (63%)
  local copies, waits for them, and re-layouts  131 us (13%)
  waiting for transfers between devices  98.6 us (10%)
  matrix products  74.6 us (7%)
  other arithmetic  34.5 us (3%)
  starting transfers between devices  20.3 us (2%)
  between operations  14.7 us (1%)
    all_gather x2, blocking collectives, on_device(): gathered = lax.all_gather(own_block, ('gx', 'gy'), axis=0, tiled=True)  652 us
    unnamed x121, local copies, waits for them, and re-layouts  98.1 us
    psum x2, waiting for transfers between devices, on_device(): totals = lax.psum(partial_value, ('gx', 'gy'))  97.8 us
    dot_general x16, matrix products, conv_rows(): jnp.einsum('otc,tcxy->oxy', shaped_weights, stacked, preferred_element_ty...  53.9 us
    convert_element_type x2, other arithmetic, on_device(): jax.nn.gelu(summed, approximate=False).astype(jnp.bfloat16)  20.9 us
  transfers between devices with their start and end apart: 10, of which 4 were waited for; matrix products, arithmetic and copies ran while one was open for 18% of the time, Pallas kernels for 0%

commit v1 on v0

--- a/solution.py
+++ b/solution.py
@@ -110,7 +110,12 @@
                 imaginary_spec.reshape(planes_here, channels, MODES),
             ]
         )
-        totals = lax.psum(partial_value, ("gx", "gy"))
+
+        def hold_streams(tile_in):
+            y = lax.all_gather(tile_in, axis_name=("gx", "gy")).sum(axis=0)
+            return y
+
+        totals = hold_streams(partial_value)
         own_modes = lax.dynamic_slice_in_dim(totals, mode_start, share_modes, 3)
 
         def mix_modes(spectrum, weights):

time: 1030 us -> 1560 us (1.51)
  waiting for transfers between devices: 98.6 us -> 535 us
  local copies, waits for them, and re-layouts: 131 us -> 185 us
  other arithmetic: 34.5 us -> 68.5 us
    all_gather x0 -> x2, waiting for transfers between devices: none -> 529 us  [hold_streams(): y = lax.all_gather(tile_in, axis_name=('gx', 'gy')).sum(axis=0)]
    psum x2 -> x0, waiting for transfers between devices: 97.8 us -> none  [on_device(): totals = lax.psum(partial_value, ('gx', 'gy'))]
    unnamed x121 -> x129, local copies, waits for them, and re-layouts: 98.1 us -> 157 us
    reduce_sum x0 -> x2, other arithmetic: none -> 35.6 us  [hold_streams(): y = lax.all_gather(tile_in, axis_name=('gx', 'gy')).sum(axis=0)]
  transfers between devices with their start and end apart: 10 -> 10, of which waited for: 4 -> 6; matrix products, arithmetic and copies ran while one was open for 18% -> 10% of each run, Pallas kernels for 0% -> 0%
where the time goes in v1:
time: 1560 us; the launch traced here: 1550 us
  blocking collectives  657 us (42%)
  waiting for transfers between devices  535 us (34%)
  local copies, waits for them, and re-layouts  185 us (12%)
  matrix products  70.6 us (5%)
  other arithmetic  68.5 us (4%)
  starting transfers between devices  19.6 us (1%)
    all_gather x2, blocking collectives, on_device(): gathered = lax.all_gather(own_block, ('gx', 'gy'), axis=0, tiled=True)  657 us
    all_gather x2, waiting for transfers between devices, hold_streams(): y = lax.all_gather(tile_in, axis_name=('gx', 'gy')).sum(axis=0)  529 us
    unnamed x129, local copies, waits for them, and re-layouts  157 us
    dot_general x16, matrix products, conv_rows(): jnp.einsum('otc,tcxy->oxy', shaped_weights, stacked, preferred_element_ty...  49.9 us
    reduce_sum x2, other arithmetic, hold_streams(): y = lax.all_gather(tile_in, axis_name=('gx', 'gy')).sum(axis=0)  35.6 us
  transfers between devices with their start and end apart: 10, of which 6 were waited for; matrix products, arithmetic and copies ran while one was open for 10% of the time, Pallas kernels for 0%

profile of v1, /device:TPU:0, one launch (start us, length us, event | category | flops | bytes accessed | tf_op | source)
XLA Modules:
  0.0 1550.5 jit_solution(7015743341356248317)
XLA Ops:
  14.5 6.1 collective-permute-start.1
  31.0 3.4 collective-permute-start.3
  37.7 3.4 collective-permute-done.2
  66.7 3.8 copy-done.18
  92.6 6.5 convolution_bitcast_fusion.9
  106.3 269.2 %all-gather.7.cloned.1.call-done = f32[256,1,20,2048]{3,1,2,0:T(1,128)} async-done(((f32[2,1,20,2048]{3,1,2,0:T(1,128)}), f32[256,1,20,2048]{3,1,2,0:T(1,128)}) %all-gather.7.cloned.1.call-update) | async-done | bytes 41943056 | tf_op jit(solution)/shard_map/all_gather | solution.py:115
  375.5 38.0 %copy.418 = f32[256,1,20,2048]{3,2,1,0:T(8,128)} copy(f32[256,1,20,2048]{3,1,2,0:T(1,128)} %all-gather.7.cloned.1.call-done) | data formatting | bytes 83886080
  413.4 17.8 %bitcast_reduce_fusion.1 = f32[2,20,2048]{2,1,0:T(8,128)S(1)} fusion(f32[128,2,20,2048]{3,2,1,0:T(8,128)} %bitcast.1571), kind=kLoop, calls=%fused_computation.1 | loop fusion | flops 10403840 | bytes 42270720 | tf_op jit(solution)/shard_map/reduce_sum | solution.py:115
  432.8 328.6 %all-gather.1 = f32[256,1,20,16]{2,3,1,0:T(8,128)S(1)} all-gather(f32[2,1,20,16]{2,3,1,0:T(8,128)S(1)} %pad_maximum_fusion.8), channel_id=3, replica_groups=mesh['gx'=16,'gy'=8] {'gx','gy'}, dimensions={0}, use_global_device_ids=true | all-gather | bytes 330240 | tf_op jit(solution)/shard_map/all_gather | solution.py:133
  767.3 3.0 convolution_bitcast_fusion.2
  770.3 10.9 fusion.42
  788.2 5.3 collective-permute-start.5
  797.7 4.3 collective-permute-start.7
  820.7 3.3 copy-done.19
  826.3 2.9 constant_dynamic-update-slice_fusion.146
  857.9 5.3 fusion.22
  863.2 5.5 fusion.19
  868.7 5.3 fusion.16
  873.9 5.3 fusion.25
  879.3 259.7 %all-gather.9.cloned.1.call-done = f32[256,1,20,2048]{3,1,2,0:T(1,128)} async-done(((f32[2,1,20,2048]{3,1,2,0:T(1,128)}), f32[256,1,20,2048]{3,1,2,0:T(1,128)}) %all-gather.9.cloned.1.call-update) | async-done | bytes 41943056 | tf_op jit(solution)/shard_map/all_gather | solution.py:115
  1139.0 38.2 %copy.419 = f32[256,1,20,2048]{3,2,1,0:T(8,128)} copy(f32[256,1,20,2048]{3,1,2,0:T(1,128)} %all-gather.9.cloned.1.call-done) | data formatting | bytes 83886080
  1177.2 17.8 %bitcast_reduce_fusion = f32[2,20,2048]{2,1,0:T(8,128)S(1)} fusion(f32[128,2,20,2048]{3,2,1,0:T(8,128)} %bitcast.1572), kind=kLoop, calls=%fused_computation | loop fusion | flops 10403840 | bytes 42270720 | tf_op jit(solution)/shard_map/reduce_sum | solution.py:115
  1196.6 328.4 %all-gather.3 = f32[256,1,20,16]{2,3,1,0:T(8,128)S(1)} all-gather(f32[2,1,20,16]{2,3,1,0:T(8,128)S(1)} %pad_maximum_fusion.9), channel_id=5, replica_groups=mesh['gx'=16,'gy'=8] {'gx','gy'}, dimensions={0}, use_global_device_ids=true | all-gather | bytes 330240 | tf_op jit(solution)/shard_map/all_gather | solution.py:133
  1531.5 10.5 fusion.54
  (262 shorter events, 152.9 us)
Async XLA Ops:
  6.5 368.9 %all-gather.7.cloned.1.call-start = ((), (), s32[]{:S(2)}) async-start(), calls=%async_computation | async-start | bytes 42270720 | tf_op jit(solution)/shard_map/all_gather | solution.py:115
  6.7 13.8 copy-start.20
  6.7 14.4 copy-start.11
  6.8 15.2 copy-start.22
  14.2 1124.8 %all-gather.9.cloned.1.call-start = ((), (), s32[]{:S(2)}) async-start(), calls=%async_computation.1 | async-start | bytes 42270720 | tf_op jit(solution)/shard_map/all_gather | solution.py:115
  14.4 13.7 collective-permute-start
  14.5 14.4 collective-permute-start.1
  31.0 10.7 collective-permute-start.3
  34.4 6.8 collective-permute-start.2
  92.6 8.9 slice-start.1
  413.4 18.3 %copy-start.4 = (f32[20,20,16]{1,2,0:T(8,128)S(1)}, f32[20,20,16]{1,2,0:T(8,128)}, u32[]{:S(2)}) copy-start(f32[20,20,16]{1,2,0:T(8,128)} %get-tuple-element.287) | copy-start | bytes 76804
  765.5 15.7 %copy-start.14 = (bf16[256,32]{0,1:T(8,128)(2,1)S(1)}, bf16[256,32]{0,1:T(8,128)(2,1)}, u32[]{:S(2)}) copy-start(bf16[256,32]{0,1:T(8,128)(2,1)} %copy-done.13) | copy-start | bytes 49156
  765.5 15.7 %copy-start.16 = (bf16[256,32]{0,1:T(8,128)(2,1)S(1)}, bf16[256,32]{0,1:T(8,128)(2,1)}, u32[]{:S(2)}) copy-start(bf16[256,32]{0,1:T(8,128)(2,1)} %copy-done.15) | copy-start | bytes 49156
  784.3 17.7 %copy-start.17 = (bf16[20,180]{1,0:T(8,128)(2,1)S(1)}, bf16[20,180]{1,0:T(8,128)(2,1)}, u32[]{:S(2)}) copy-start(bf16[20,180]{1,0:T(8,128)(2,1)} %get-tuple-element.7) | copy-start | bytes 21604
  784.3 17.8 %copy-start.12 = (bf16[20,500]{1,0:T(8,128)(2,1)S(1)}, bf16[20,500]{1,0:T(8,128)(2,1)}, u32[]{:S(2)}) copy-start(bf16[20,500]{1,0:T(8,128)(2,1)} %get-tuple-element.5) | copy-start | bytes 60004
  788.1 7.1 collective-permute-start.4
  788.2 7.2 collective-permute-start.5
  797.1 6.4 collective-permute-start.6
  797.7 6.3 collective-permute-start.7
  1177.2 18.0 %copy-start.2 = (f32[20,20,16]{1,2,0:T(8,128)S(1)}, f32[20,20,16]{1,2,0:T(8,128)}, u32[]{:S(2)}) copy-start(f32[20,20,16]{1,2,0:T(8,128)} %get-tuple-element.285) | copy-start | bytes 76804
  1177.2 18.3 %copy-start.3 = (f32[20,20,16]{1,2,0:T(8,128)S(1)}, f32[20,20,16]{1,2,0:T(8,128)}, u32[]{:S(2)}) copy-start(f32[20,20,16]{1,2,0:T(8,128)} %get-tuple-element.288) | copy-start | bytes 76804
  1195.0 334.2 %copy-start.8 = (f32[32,256]{1,0:T(8,128)S(1)}, f32[32,256]{1,0:T(8,128)}, u32[]{:S(2)}) copy-start(f32[32,256]{1,0:T(8,128)} %get-tuple-element.295) | copy-start | bytes 98308
  1195.0 334.2 %copy-start.9 = (f32[32,256]{1,0:T(8,128)S(1)}, f32[32,256]{1,0:T(8,128)}, u32[]{:S(2)}) copy-start(f32[32,256]{1,0:T(8,128)} %get-tuple-element.296) | copy-start | bytes 98308
  1196.6 334.9 %copy-start.21 = (f32[20]{0:T(128)S(1)}, f32[20]{0:T(128)}, u32[]{:S(2)}) copy-start(f32[20]{0:T(128)} %get-tuple-element.299) | copy-start | bytes 244
  (14 other events, 78.2 us)
Sparse Core Ops, SparseCore 0:
  14.3 361.0 all-gather.6
  787.0 351.9 all-gather.8
